TPU v7x, 32 devices: a whole 2x2x4 slice. The times are simulated.
32 devices in a mesh: req: 8 (over z, y), tp: 4 (over x, core).
Axes of the slice: x: 2, y: 2, z: 4, core: 2. Of those that a mesh axis runs over, the one named last changes fastest.
Arguments:
- residual: bfloat16 [256, 2048], P('req'), may hold values from -6 to 6
- cache_lengths: int32 [256], P('req'), may hold values from 4 to 4096, as said below
- input_gain: float32 [2048], replicated, may hold values from 0.1 to 1.9
- inner_weight: bfloat16 [2048, 2, 1536], P(None, None, 'tp'), may hold values from -0.125 to 0.125
- step_weight: bfloat16 [2048, 24], P(None, 'tp'), may hold values from -0.125 to 0.125
- step_bias: float32 [24], P('tp'), may hold values from -4 to -1
- decay_log: float32 [24], P('tp'), may hold values from 0 to 2.77
- skip_gain: float32 [24], P('tp'), may hold values from 0.5 to 2
- conv_weight: bfloat16 [4, 1536], P(None, 'tp'), may hold values from -3 to 3
- conv_state: bfloat16 [256, 3, 1536], P('req', None, 'tp'), may hold values from -6 to 6
- coupling_weight: bfloat16 [2048, 512], P(None, 'tp'), may hold values from -0.125 to 0.125
- coupling_conv: bfloat16 [4, 512], P(None, 'tp'), may hold values from -3 to 3
- coupling_state: bfloat16 [256, 3, 512], P('req', None, 'tp'), may hold values from -6 to 6
- scan_state: bfloat16 [256, 24, 64, 256], P('req', 'tp'), may hold values from -30 to 30
- mixer_gain: float32 [1536], P('tp'), may hold values from 0.1 to 1.9
- attention_weight: bfloat16 [2048, 1536], P(None, 'tp'), may hold values from -0.125 to 0.125
- sink_cache: bfloat16 [256, 4, 512], P('req'), may hold values from -2000 to 2000
- window_cache: bfloat16 [256, 1024, 512], P('req', 'tp'), may hold values from -9 to 9
- mamba_out: bfloat16 [1536, 2048], P('tp'), may hold values from -0.15625 to 0.15625
- attention_out: bfloat16 [1024, 2048], P('tp'), may hold values from -0.5 to 0.5
- final_gain: float32 [2048], replicated, may hold values from 0.1 to 1.9
- output_head: bfloat16 [2048, 65536], P(None, ('req', 'tp')), may hold values from -0.375 to 0.375
Outputs:
- new_residual: bfloat16 [256, 2048], P('req', 'tp')
- logits: float32 [256, 65536], P(('req', 'tp'))
- new_scan_state: bfloat16 [256, 24, 64, 256], P('req', 'tp')
- new_conv_state: bfloat16 [256, 3, 1536], P('req', None, 'tp')
- new_coupling_state: bfloat16 [256, 3, 512], P('req', None, 'tp')
- new_key_value: bfloat16 [256, 512], P('req')
Inputs may be any that keep to these rules, and one draw needn't show every extreme that they name: `cache_lengths`: A request's cache holds positions 0 to its length - 1; the new token stands at the position equal to the length. Some request has length exactly 4096.
All inputs are finite; a program needn't handle non-finite values.
Results may differ from a plain program's by a relative error of at most 0.02.
Values may be sent and summed in bfloat16 or wider, within the bound.
A program may use at most 128 MiB of HBM per device.

v0:
```python
import jax
import jax.numpy as jnp
from jax import lax
from jax.sharding import PartitionSpec as P

MH = 24
MP = 64
NS = 256
QH = 8
KVH = 2
HD = 128
WIN = 1024
SINK = 4
EPSILON = 1e-05
NEG_BIG = -1e30


def combined_all(array, axis, combine):
    everything = jax.tree.map(
        lambda part, kind: lax.all_gather(part.astype(kind), axis),
        array,
        (jnp.bfloat16, jnp.bfloat16, jnp.bfloat16),
    )

    def take(k):
        return jax.tree.map(lambda part, own: part[k].astype(own.dtype), everything, array)

    return lax.fori_loop(
        1, lax.axis_size(axis), lambda k, so_far: combine(so_far, take(k)), take(0)
    )


def norm_rows(values, gain):
    widened = values.astype(jnp.float32)
    mean_sq = jnp.mean(widened * widened, axis=-1, keepdims=True)
    return (widened * lax.rsqrt(mean_sq + EPSILON) * gain).astype(jnp.bfloat16)


def conv_apply(old_state, fresh_row, taps):
    window = jnp.concatenate([old_state, fresh_row[:, None, :]], axis=1)
    mixed_rows = jnp.einsum("rkc,kc->rc", window, taps, preferred_element_type=jnp.float32)
    return (jax.nn.silu(mixed_rows), window[:, 1:, :])


def merge_parts(first_part, second_part):
    first_peak, first_total, first_sum = first_part
    second_peak, second_total, second_sum = second_part
    row_peak = jnp.maximum(first_peak, second_peak)
    first_scale = jnp.exp(first_peak - row_peak)
    second_scale = jnp.exp(second_peak - row_peak)
    return (
        row_peak,
        first_total * first_scale + second_total * second_scale,
        first_sum * first_scale[..., None] + second_sum * second_scale[..., None],
    )


def attend_part(queries, key_rows, value_rows, valid_mask):
    scores = jnp.einsum(
        "rkgd,rskd->rkgs", queries, key_rows, preferred_element_type=jnp.float32
    ) * HD ** (-0.5)
    masked = jnp.where(valid_mask, scores, NEG_BIG)
    row_peak = jnp.max(masked, axis=-1)
    weights = jnp.where(valid_mask, jnp.exp(masked - row_peak[..., None]), 0.0)
    totals = jnp.sum(weights, axis=-1)
    summed = jnp.einsum(
        "rkgs,rskd->rkgd",
        weights.astype(jnp.bfloat16),
        value_rows,
        preferred_element_type=jnp.float32,
    )
    return (row_peak, totals, summed)


def body(
    residual,
    cache_lengths,
    input_gain,
    inner_weight,
    step_weight,
    step_bias,
    decay_log,
    skip_gain,
    conv_weight,
    conv_state,
    coupling_weight,
    coupling_conv,
    coupling_state,
    scan_state,
    mixer_gain,
    attention_weight,
    sink_cache,
    window_cache,
    mamba_out,
    attention_out,
    final_gain,
    output_head,
):
    row_count = residual.shape[0]
    tp_size = lax.axis_size("tp")
    tp_index = lax.axis_index("tp")
    local_heads = scan_state.shape[1]
    local_units = inner_weight.shape[2]
    half_width = KVH * HD
    group_size = QH // KVH
    normed = norm_rows(residual, input_gain)
    projected = jnp.einsum(
        "rd,dtc->rtc", normed, inner_weight, preferred_element_type=jnp.float32
    ).astype(jnp.bfloat16)
    gate_rows = lax.optimization_barrier(projected[:, 0, :])
    x_rows, new_conv_state = conv_apply(conv_state, projected[:, 1, :], conv_weight)
    step_rows = lax.optimization_barrier(
        jnp.dot(normed, step_weight, preferred_element_type=jnp.float32).astype(jnp.bfloat16)
    )
    step_size = jax.nn.softplus(step_rows.astype(jnp.float32) + step_bias)
    decay_rate = jnp.exp(-step_size * jnp.exp(decay_log))
    coupling_pre = jnp.dot(normed, coupling_weight, preferred_element_type=jnp.float32).astype(
        jnp.bfloat16
    )
    coupling_rows, new_coupling_state = conv_apply(coupling_state, coupling_pre, coupling_conv)
    qkv_local = jnp.dot(normed, attention_weight, preferred_element_type=jnp.float32).astype(
        jnp.bfloat16
    )
    qkv_rows, coupling_all = (
        lax.all_gather(qkv_local, "tp", axis=1, tiled=True),
        lax.all_gather(coupling_rows.astype(jnp.bfloat16), "tp", axis=1, tiled=True),
    )
    input_vec = coupling_all[:, :NS].astype(jnp.float32)
    output_vec = coupling_all[:, NS:].astype(jnp.float32)
    x_heads = x_rows.reshape(row_count, local_heads, MP)
    updated = (
        decay_rate[:, :, None, None] * scan_state.astype(jnp.float32)
        + (step_size[:, :, None] * x_heads)[:, :, :, None] * input_vec[:, None, None, :]
    )
    readout = (
        jnp.einsum("rhpn,rn->rhp", updated, output_vec, precision=lax.Precision.HIGHEST)
        + skip_gain[None, :, None] * x_heads
    )
    new_scan_state = updated.astype(jnp.bfloat16)
    gated_rows = readout.reshape(row_count, local_units) * jax.nn.silu(
        gate_rows.astype(jnp.float32)
    )
    square_total = lax.psum(jnp.sum(gated_rows * gated_rows, axis=1), "tp")
    mamba_rows = (
        gated_rows * lax.rsqrt(square_total / (MH * MP) + EPSILON)[:, None] * mixer_gain
    ).astype(jnp.bfloat16)
    queries = qkv_rows[:, : QH * HD].reshape(row_count, KVH, group_size, HD)
    fresh_keys = qkv_rows[:, QH * HD : QH * HD + half_width].reshape(row_count, 1, KVH, HD)
    fresh_values = qkv_rows[:, QH * HD + half_width :].reshape(row_count, 1, KVH, HD)
    new_key_value = qkv_rows[:, QH * HD :]
    is_lead = tp_index == 0
    sink_keys = sink_cache[:, :, :half_width].reshape(row_count, SINK, KVH, HD)
    sink_values = sink_cache[:, :, half_width:].reshape(row_count, SINK, KVH, HD)
    sink_part = attend_part(
        queries, sink_keys, sink_values, jnp.broadcast_to(is_lead, (row_count, 1, 1, SINK))
    )
    fresh_part = attend_part(
        queries, fresh_keys, fresh_values, jnp.broadcast_to(is_lead, (row_count, 1, 1, 1))
    )
    window_slots = window_cache.shape[1]
    slot_offset = tp_index * window_slots
    length_column = cache_lengths[:, None]
    cycle_keys = window_cache[:, :, :half_width].reshape(row_count, window_slots, KVH, HD)
    cycle_values = window_cache[:, :, half_width:].reshape(row_count, window_slots, KVH, HD)
    slot_index = slot_offset + jnp.arange(window_slots, dtype=jnp.int32)
    back_steps = (length_column - 1 - slot_index[None, :]) % WIN
    position = length_column - 1 - back_steps
    live_mask = ((position >= SINK) & (back_steps != WIN - 1))[:, None, None, :]
    cycle_part = attend_part(queries, cycle_keys, cycle_values, live_mask)
    local_peak, local_total, local_sum = merge_parts(merge_parts(sink_part, fresh_part), cycle_part)
    row_peak, totals, summed = combined_all((local_peak, local_total, local_sum), "tp", merge_parts)
    attended = (summed / totals[..., None]).reshape(row_count, QH * HD).astype(jnp.bfloat16)
    head_columns = QH // tp_size * HD
    own_heads = lax.dynamic_slice_in_dim(attended, tp_index * head_columns, head_columns, 1)
    mixed_rows = jnp.dot(mamba_rows, mamba_out, preferred_element_type=jnp.float32) + jnp.dot(
        own_heads, attention_out, preferred_element_type=jnp.float32
    )
    share_width = residual.shape[1] // tp_size
    mixed_total = lax.psum(mixed_rows.astype(jnp.bfloat16), "tp").astype(jnp.float32)
    new_full = (residual.astype(jnp.float32) + mixed_total).astype(jnp.bfloat16)
    new_residual = lax.dynamic_slice_in_dim(new_full, tp_index * share_width, share_width, 1)
    final_rows = norm_rows(new_full, final_gain)
    vocab_logits = jnp.dot(
        lax.all_gather(final_rows, "req", axis=0, tiled=True),
        output_head,
        preferred_element_type=jnp.float32,
    )
    logits = lax.all_to_all(
        vocab_logits.astype(jnp.bfloat16), ("req", "tp"), split_axis=0, concat_axis=1, tiled=True
    ).astype(vocab_logits.dtype)
    return (new_residual, logits, new_scan_state, new_conv_state, new_coupling_state, new_key_value)


def solution(mesh):
    return jax.shard_map(
        body,
        mesh=mesh,
        in_specs=(
            P("req", None),
            P("req"),
            P(),
            P(None, None, "tp"),
            P(None, "tp"),
            P("tp"),
            P("tp"),
            P("tp"),
            P(None, "tp"),
            P("req", None, "tp"),
            P(None, "tp"),
            P(None, "tp"),
            P("req", None, "tp"),
            P("req", "tp", None, None),
            P("tp"),
            P(None, "tp"),
            P("req", None, None),
            P("req", "tp", None),
            P("tp", None),
            P("tp", None),
            P(),
            P(None, ("req", "tp")),
        ),
        out_specs=(
            P("req", "tp"),
            P(("req", "tp"), None),
            P("req", "tp", None, None),
            P("req", None, "tp"),
            P("req", None, "tp"),
            P("req", None),
        ),
        check_vma=False,
    )
```

profile of v0, /device:TPU:0, one launch (start us, length us, event | category | flops | bytes accessed | tf_op | source)
XLA Modules:
  0.0 261.5 jit_solution(11709163570320856122)
XLA Ops:
  7.2 1.2 fusion.24
  8.4 1.9 convolution_convert_fusion.1
  10.3 6.3 %all_gather.24 = bf16[32,1536]{1,0:T(8,128)(2,1)S(1)} all-gather(bf16[32,384]{1,0:T(8,128)(2,1)S(1)} %convolution_convert_fusion.1), channel_id=1, replica_groups=mesh['req'=8,'tp'=4] {'tp'}, dimensions={1}, use_global_device_ids=true | all-gather | bytes 122880 | tf_op jit(solution)/shard_map/all_gather | solution.py:125
  18.6 6.0 %fusion.79 = (bf16[32,256,256]{2,1,0:T(8,128)(2,1)}, bf16[32,256,256]{2,1,0:T(8,128)(2,1)}) fusion(bf16[32,256,512]{2,1,0:T(8,128)(2,1)} %param.41), kind=kLoop, calls=%fused_computation.140 | loop fusion | bytes 16777216 | tf_op jit(solution)/shard_map/slice | solution.py:164
  24.6 6.5 %copy.137 = bf16[32,256,256]{1,2,0:T(8,128)(2,1)} copy(bf16[32,256,256]{2,1,0:T(8,128)(2,1)} %get-tuple-element.233) | data formatting | bytes 8388608
  31.2 2.9 %fusion.80 = (f32[32,2,4]{2,1,0:T(2,128)S(1)}, f32[32,2,4,256]{3,2,1,0:T(4,128)S(1)}) fusion(bf16[32,2,4,128]{3,2,1,0:T(4,128)(2,1)S(1)} %reshape.220, bf16[32,256,2,128]{1,3,2,0:T(8,128)(2,1)} %bitcast.108, pred[32,256]{1,0:T(8,128)(4,1)S(1)} %fusion.52), kind=kOutput, calls=%fused_computation.141 | convolution fusion | flops 16973568 | bytes 4531200 | tf_op jit(solution)/shard_map/rkgd,rskd->rkgs/dot_general | solution.py:59
  35.8 1.4 copy.96
  37.2 1.7 fusion.38
  38.9 1.0 copy.84
  39.9 1.3 reshape.257
  41.3 1.6 fusion.81
  44.3 1.3 max.53
  45.6 1.3 add_convert_fusion
  51.2 1.4 copy.105
  52.6 6.5 %copy.138 = bf16[32,256,256]{1,2,0:T(8,128)(2,1)} copy(bf16[32,256,256]{2,1,0:T(8,128)(2,1)} %get-tuple-element.232) | data formatting | bytes 8388608
  59.1 1.4 fusion.15
  61.4 2.2 fusion.16
  63.6 6.4 %all-gather.2 = bf16[128,2,4,128]{3,2,1,0:T(4,128)(2,1)S(1)} all-gather(bf16[32,2,4,128]{3,2,1,0:T(4,128)(2,1)S(1)} %fusion.16), channel_id=4, replica_groups=mesh['req'=8,'tp'=4] {'tp'}, dimensions={0}, use_global_device_ids=true | all-gather | bytes 327680 | tf_op jit(solution)/shard_map/all_gather | solution.py:20
  71.4 5.4 %all-gather.1 = bf16[128,2,4]{2,1,0:T(2,128)(2,1)S(1)} all-gather(bf16[32,2,4]{2,1,0:T(2,128)(2,1)} %copy.97), channel_id=3, replica_groups=mesh['req'=8,'tp'=4] {'tp'}, dimensions={0}, use_global_device_ids=true | all-gather | bytes 2560 | tf_op jit(solution)/shard_map/all_gather | solution.py:20
  79.0 1.4 copy.90
  80.4 5.4 %all-gather = bf16[128,2,4]{2,1,0:T(2,128)(2,1)S(1)} all-gather(bf16[32,2,4]{2,1,0:T(2,128)(2,1)} %copy.90), channel_id=2, replica_groups=mesh['req'=8,'tp'=4] {'tp'}, dimensions={0}, use_global_device_ids=true | all-gather | bytes 2560 | tf_op jit(solution)/shard_map/all_gather | solution.py:20
  86.5 1.4 copy.108
  88.6 8.4 %while.19 = (s32[]{:T(128)}, f32[32,2,4]{0,2,1:T(4,128)}, f32[32,2,4]{0,2,1:T(4,128)S(1)}, f32[32,2,4,128]{3,2,1,0:T(4,128)S(1)}, bf16[4,32,2,4]{1,3,2,0:T(4,128...) while((s32[]{:T(128)}, f32[32,2,4]{0,2,1:T(4,128)}, ...), condition=%wide.region_8.9_spmd, body=%wide.region_7.8_spmd.sunk | while | flops 133125 | bytes 341143 | solution.py:28
  88.6 1.3 fusion.98
  90.1 1.3 fusion.99
  91.4 1.3 fusion.98
  92.9 1.3 fusion.99
  94.2 1.3 fusion.98
  95.7 1.3 fusion.99
  99.3 1.4 fusion.17
  103.0 1.0 convolution_convert_fusion.3
  106.1 1.3 fusion.20
  108.9 5.2 %all_gather.23 = bf16[32,512]{1,0:T(8,128)(2,1)S(1)} all-gather(bf16[32,128]{1,0:T(8,128)(2,1)S(1)} %fusion.61), channel_id=1, replica_groups=mesh['req'=8,'tp'=4] {'tp'}, dimensions={1}, use_global_device_ids=true | all-gather | bytes 40960 | tf_op jit(solution)/shard_map/all_gather | solution.py:126
  116.2 10.6 %fusion.4 = f32[32,1,6,64]{3,1,2,0:T(1,128)S(1)} fusion(bf16[32,6,64,256]{3,2,1,0:T(8,128)(2,1)} %param.37, f32[32,256]{1,0:T(8,128)} %get-tuple-element.239, f32[32,6,64]{2,1,0:T(8,128)S(1)} %broadcast_multiply_fusion, f32[32,6]{1,0:T(8,128)} %copy.81, bf16[32,256,1,1]{1,0,2,3:T(8,128)(2,1)} %get-tuple-element.238), kind=kOutput, calls=%fused_computation.10 | convolution fusion | flops 50331648 | bytes 6439680 | tf_op jit(solution)/shard_map/rhpn,rn->rhp/dot_general | solution.py:136
  127.5 1.0 reshape.219
  128.7 7.4 %psum.14 = f32[32]{0:T(128)S(1)} all-reduce(f32[32]{0:T(128)S(1)} %multiply_reduce_fusion.2), channel_id=1, replica_groups=mesh['req'=8,'tp'=4] {'tp'}, use_global_device_ids=true, to_apply=%region_2.3 | all-reduce | flops 32 | bytes 256 | tf_op jit(solution)/shard_map/psum | solution.py:143
  136.1 1.8 fusion.54
  137.9 2.2 fusion.11
  140.2 31.8 %all-reduce.2.cloned.1.call-done = bf16[32,2048]{1,0:T(8,128)(2,1)} async-done(((bf16[32,2048]{1,0:T(8,128)(2,1)}), bf16[32,2048]{1,0:T(8,128)(2,1)}) %all-reduce.2.cloned.1.call-update) | async-done | bytes 131088 | tf_op jit(solution)/shard_map/psum | solution.py:179
  172.0 1.1 fusion.21
  173.9 41.2 %all-gather.5.cloned.1.call-done = bf16[256,2048]{1,0:T(8,128)(2,1)} async-done(((bf16[32,2048]{1,0:T(8,128)(2,1)}), bf16[256,2048]{1,0:T(8,128)(2,1)}) %all-gather.5.cloned.1.call-update) | async-done | bytes 1048592 | tf_op jit(solution)/shard_map/all_gather | solution.py:184
  215.1 7.0 %fusion.10 = bf16[32,8,2048]{2,1,0:T(8,128)(2,1)} fusion(bf16[256,2048]{1,0:T(8,128)(2,1)} %all-gather.5.cloned.1.call-done, bf16[2048,2048]{1,0:T(8,128)(2,1)} %param.45), kind=kOutput, calls=%fused_computation.17 | convolution fusion | flops 2148007936 | bytes 10485760 | tf_op jit(solution)/shard_map/dot_general | solution.py:183
  222.1 3.5 %all-to-all-start = ((bf16[32,8,2048]{2,1,0:T(8,128)(2,1)}), bf16[32,8,2048]{2,1,0:T(8,128)(2,1)}, u32[]{:S(2)}, u32[]{:S(2)}) async-start(bf16[32,8,2048]{2,1,0:T(8,128)(2,1)} %fusion.10), calls=%async_computation | async-start | bytes 2097152 | tf_op jit(solution)/shard_map/all_to_all | solution.py:188
  225.6 1.4 slice.85
  227.0 1.3 fusion.53
  229.0 8.1 %fusion.3 = bf16[32,6,64,256]{3,2,1,0:T(8,128)(2,1)} fusion(bf16[32,6,64,256]{3,2,1,0:T(8,128)(2,1)} %param.37, f32[32,256]{1,0:T(8,128)S(1)} %copy-done.11, f32[32,6,64]{2,1,0:T(8,128)S(1)} %copy-done.7, f32[32,6]{1,0:T(8,128)} %copy.81), kind=kLoop, calls=%fused_computation.9 | loop fusion | flops 15728640 | bytes 12665600 | tf_op jit(solution)/shard_map/convert_element_type | solution.py:139
  237.7 14.2 %all-to-all-done = bf16[32,8,2048]{2,1,0:T(8,128)(2,1)} async-done(((bf16[32,8,2048]{2,1,0:T(8,128)(2,1)}), bf16[32,8,2048]{2,1,0:T(8,128)(2,1)}, u32[]{:S(2)}, u32[]{:S(2)}) %all-to-all-start) | async-done | bytes 1048608 | tf_op jit(solution)/shard_map/all_to_all | solution.py:188
  251.8 2.8 %convert_element_type.203 = f32[32,8,2048]{2,1,0:T(8,128)} convert(bf16[32,8,2048]{2,1,0:T(8,128)(2,1)} %all-to-all-done) | non-fusion elementwise | flops 524288 | bytes 3145728 | tf_op jit(solution)/shard_map/convert_element_type | solution.py:190
  (106 shorter events, 29.2 us)
Async XLA Ops:
  7.2 92.1 %copy-start = (bf16[2048,2,384]{2,1,0:T(2,128)(2,1)S(1)}, bf16[2048,2,384]{2,1,0:T(2,128)(2,1)}, u32[]{:S(2)}) copy-start(bf16[2048,2,384]{2,1,0:T(2,128)(2,1)} %param.27) | copy-start | bytes 9437188
  7.2 164.8 %all-reduce.2.cloned.1.call-start = ((), (), s32[]{:S(2)}) async-start(), calls=%async_computation.1 | async-start | bytes 262144 | tf_op jit(solution)/shard_map/psum | solution.py:179
  8.4 8.2 %copy-start.20 = (f32[32]{0:T(128)}, f32[32]{0:T(128)S(1)}, u32[]{:S(2)}) copy-start(f32[32]{0:T(128)S(1)} %add_rsqrt_fusion.2) | copy-start | bytes 388
  16.6 0.7 copy-start.5
  31.2 6.0 %copy-start.14 = (pred[32,256]{1,0:T(8,128)(4,1)}, pred[32,256]{1,0:T(8,128)(4,1)S(1)}, u32[]{:S(2)}) copy-start(pred[32,256]{1,0:T(8,128)(4,1)S(1)} %fusion.52) | copy-start | bytes 24580
  34.2 24.9 %copy-start.4 = (f32[32,2,4,256]{3,2,1,0:T(4,128)}, f32[32,2,4,256]{3,2,1,0:T(4,128)S(1)}, u32[]{:S(2)}) copy-start(f32[32,2,4,256]{3,2,1,0:T(4,128)S(1)} %get-tuple-element.246) | copy-start | bytes 786436
  51.2 7.9 %copy-start.16 = (f32[32,2,4]{2,1,0:T(2,128)S(1)}, f32[32,2,4]{2,1,0:T(2,128)}, u32[]{:S(2)}) copy-start(f32[32,2,4]{2,1,0:T(2,128)} %copy.100) | copy-start | bytes 3076
  52.6 7.9 %copy-start.15 = (pred[32,256]{1,0:T(8,128)(4,1)S(1)}, pred[32,256]{1,0:T(8,128)(4,1)}, u32[]{:S(2)}) copy-start(pred[32,256]{1,0:T(8,128)(4,1)} %copy-done.14) | copy-start | bytes 24580
  59.1 2.3 copy-start.1
  59.1 2.3 copy-start.17
  59.1 11.5 %copy-start.19 = (bf16[32,2,4]{0,2,1:T(4,128)(2,1)S(1)}, bf16[32,2,4]{0,2,1:T(4,128)(2,1)}, u32[]{:S(2)}) copy-start(bf16[32,2,4]{0,2,1:T(4,128)(2,1)} %get-tuple-element.228) | copy-start | bytes 1540
  60.5 38.8 %copy-start.2 = (bf16[32,2048]{1,0:T(8,128)(2,1)S(1)}, bf16[32,2048]{1,0:T(8,128)(2,1)}, u32[]{:S(2)}) copy-start(bf16[32,2048]{1,0:T(8,128)(2,1)} %param.24) | copy-start | bytes 393220
  63.6 37.8 %copy-start.8 = (bf16[32,3,384]{2,0,1:T(8,128)(2,1)S(1)}, bf16[32,3,384]{2,0,1:T(8,128)(2,1)}, u32[]{:S(2)}) copy-start(bf16[32,3,384]{2,0,1:T(8,128)(2,1)} %param.33) | copy-start | bytes 221188
  69.9 0.7 copy-start.3
  100.7 26.1 %copy-start.9 = (bf16[32,1,384]{2,0,1:T(8,128)(2,1)}, bf16[32,1,384]{2,0,1:T(8,128)(2,1)S(1)}, u32[]{:S(2)}) copy-start(bf16[32,1,384]{2,0,1:T(8,128)(2,1)S(1)} %get-tuple-element.237) | copy-start | bytes 73732
  107.4 19.4 %copy-start.12 = (bf16[32,1,128]{2,0,1:T(8,128)(2,1)}, bf16[32,1,128]{2,0,1:T(8,128)(2,1)S(1)}, u32[]{:S(2)}) copy-start(bf16[32,1,128]{2,0,1:T(8,128)(2,1)S(1)} %fusion.20) | copy-start | bytes 24580
  116.2 10.6 %copy-start.6 = (f32[32,6,64]{2,1,0:T(8,128)}, f32[32,6,64]{2,1,0:T(8,128)S(1)}, u32[]{:S(2)}) copy-start(f32[32,6,64]{2,1,0:T(8,128)S(1)} %broadcast_multiply_fusion) | copy-start | bytes 147460
  116.2 10.6 %copy-start.22 = (f32[6]{0:T(128)S(1)}, f32[6]{0:T(128)}, u32[]{:S(2)}) copy-start(f32[6]{0:T(128)} %param.31) | copy-start | bytes 76
  116.2 19.9 %copy-start.21 = (f32[384]{0:T(512)S(1)}, f32[384]{0:T(512)}, u32[]{:S(2)}) copy-start(f32[384]{0:T(512)} %param.38) | copy-start | bytes 4612
  116.2 56.9 %copy-start.18 = (f32[2048]{0:T(1024)S(1)}, f32[2048]{0:T(1024)}, u32[]{:S(2)}) copy-start(f32[2048]{0:T(1024)} %param.44) | copy-start | bytes 24580
  140.1 75.0 %all-gather.5.cloned.1.call-start = ((), (), s32[]{:S(2)}) async-start(), calls=%async_computation.2 | async-start | bytes 1179648 | tf_op jit(solution)/shard_map/all_gather | solution.py:184
  173.9 53.1 %copy-start.13 = (bf16[32,1,128]{2,0,1:T(8,128)(2,1)S(1)}, bf16[32,1,128]{2,0,1:T(8,128)(2,1)}, u32[]{:S(2)}) copy-start(bf16[32,1,128]{2,0,1:T(8,128)(2,1)} %copy-done.12) | copy-start | bytes 24580
  173.9 54.5 %copy-start.10 = (bf16[32,1,384]{2,0,1:T(8,128)(2,1)S(1)}, bf16[32,1,384]{2,0,1:T(8,128)(2,1)}, u32[]{:S(2)}) copy-start(bf16[32,1,384]{2,0,1:T(8,128)(2,1)} %copy-done.9) | copy-start | bytes 73732
  173.9 55.1 %copy-start.7 = (f32[32,6,64]{2,1,0:T(8,128)S(1)}, f32[32,6,64]{2,1,0:T(8,128)}, u32[]{:S(2)}) copy-start(f32[32,6,64]{2,1,0:T(8,128)} %copy-done.6) | copy-start | bytes 147460
  173.9 55.1 %copy-start.11 = (f32[32,256]{1,0:T(8,128)S(1)}, f32[32,256]{1,0:T(8,128)}, u32[]{:S(2)}) copy-start(f32[32,256]{1,0:T(8,128)} %get-tuple-element.239) | copy-start | bytes 98308
  222.1 29.7 %all-to-all-start = ((bf16[32,8,2048]{2,1,0:T(8,128)(2,1)}), bf16[32,8,2048]{2,1,0:T(8,128)(2,1)}, u32[]{:S(2)}, u32[]{:S(2)}) async-start(bf16[32,8,2048]{2,1,0:T(8,128)(2,1)} %fusion.10), calls=%async_computation | async-start | bytes 2097152 | tf_op jit(solution)/shard_map/all_to_all | solution.py:188
Sparse Core Ops, SparseCore 0:
  140.2 31.7 all-reduce.1
  174.9 40.1 all-gather.4
where the time goes:
time: 264 us; the launch traced here: 261 us
  waiting for transfers between devices  87.2 us (33%)
  local copies, waits for them, and re-layouts  46.1 us (17%)
  other arithmetic  37.1 us (14%)
  matrix products  37 us (14%)
  blocking collectives  36.1 us (14%)
  between operations  14.4 us (5%)
  starting transfers between devices  3.56 us (1%)
    all_gather x1, waiting for transfers between devices, body(): lax.all_gather(final_rows, 'req', axis=0, tiled=True)  41.2 us
    psum x1, waiting for transfers between devices, body(): lax.psum(mixed_rows.astype(jnp.bfloat16), 'tp').astype(jnp.float32)  31.8 us
    all_gather x3, blocking collectives, combined_all(): lax.all_gather(part.astype(kind), axis)  17.2 us
    unnamed x48, local copies, waits for them, and re-layouts  15.3 us
    all_to_all x1, waiting for transfers between devices, body(): lax.all_to_all(vocab_logits.astype(jnp.bfloat16), ('req', 'tp'), split_ax...  14.2 us
    dot_general x1, matrix products, body(): jnp.einsum('rhpn,rn->rhp', updated, output_vec, precision=lax.Precision.H...  10.6 us
    convert_element_type x1, other arithmetic, body(): new_scan_state = updated.astype(jnp.bfloat16)  8.08 us
    psum x1, blocking collectives, body(): square_total = lax.psum(jnp.sum(gated_rows * gated_rows, axis=1), 'tp')  7.38 us
  transfers between devices with their start and end apart: 3, of which 3 were waited for; matrix products, arithmetic and copies ran while one was open for 5% of the time, Pallas kernels for 0%

commit v1 on v0

--- a/solution.py
+++ b/solution.py
@@ -185,8 +185,16 @@
         output_head,
         preferred_element_type=jnp.float32,
     )
-    logits = lax.all_to_all(
-        vocab_logits.astype(jnp.bfloat16), ("req", "tp"), split_axis=0, concat_axis=1, tiled=True
+    logits = jnp.concatenate(
+        lax.all_to_all(
+            jnp.stack(
+                jnp.split(vocab_logits.astype(jnp.bfloat16), lax.axis_size(("req", "tp")), axis=0)
+            ),
+            ("req", "tp"),
+            0,
+            0,
+        ),
+        axis=1,
     ).astype(vocab_logits.dtype)
     return (new_residual, logits, new_scan_state, new_conv_state, new_coupling_state, new_key_value)
 

time: 264 us -> 283 us (1.072)
  local copies, waits for them, and re-layouts: 46.1 us -> 65.8 us
    unnamed x48 -> x79, local copies, waits for them, and re-layouts: 15.3 us -> 34.4 us
  transfers between devices with their start and end apart: 3 -> 3, of which waited for: 3 -> 3; matrix products, arithmetic and copies ran while one was open for 5% -> 4% of each run, Pallas kernels for 0% -> 0%
where the time goes in v1:
time: 283 us; the launch traced here: 280 us
  waiting for transfers between devices  87.2 us (31%)
  local copies, waits for them, and re-layouts  65.8 us (23%)
  other arithmetic  37.1 us (13%)
  blocking collectives  36.1 us (13%)
  matrix products  36 us (13%)
  between operations  14.4 us (5%)
  starting transfers between devices  3.56 us (1%)
    all_gather x1, waiting for transfers between devices, body(): lax.all_gather(final_rows, 'req', axis=0, tiled=True)  41.2 us
    unnamed x79, local copies, waits for them, and re-layouts  34.4 us
    psum x1, waiting for transfers between devices, body(): lax.psum(mixed_rows.astype(jnp.bfloat16), 'tp').astype(jnp.float32)  31.8 us
    all_gather x3, blocking collectives, combined_all(): lax.all_gather(part.astype(kind), axis)  17.2 us
    all_to_all x1, waiting for transfers between devices, body(): lax.all_to_all(jnp.stack(jnp.split(vocab_logits.astype(jnp.bfloat16), lax...  14.2 us
    dot_general x1, matrix products, body(): jnp.einsum('rhpn,rn->rhp', updated, output_vec, precision=lax.Precision.H...  10.6 us
    convert_element_type x1, other arithmetic, body(): new_scan_state = updated.astype(jnp.bfloat16)  8.08 us
    psum x1, blocking collectives, body(): square_total = lax.psum(jnp.sum(gated_rows * gated_rows, axis=1), 'tp')  7.38 us
  transfers between devices with their start and end apart: 3, of which 3 were waited for; matrix products, arithmetic and copies ran while one was open for 4% of the time, Pallas kernels for 0%

profile of v1, /device:TPU:0, one launch (start us, length us, event | category | flops | bytes accessed | tf_op | source)
XLA Modules:
  0.0 280.2 jit_solution(2752281246695487277)
XLA Ops:
  7.2 1.2 fusion.23
  8.4 1.9 convolution_convert_fusion.1
  10.3 6.3 %all_gather.24 = bf16[32,1536]{1,0:T(8,128)(2,1)S(1)} all-gather(bf16[32,384]{1,0:T(8,128)(2,1)S(1)} %convolution_convert_fusion.1), channel_id=1, replica_groups=mesh['req'=8,'tp'=4] {'tp'}, dimensions={1}, use_global_device_ids=true | all-gather | bytes 122880 | tf_op jit(solution)/shard_map/all_gather | solution.py:125
  18.6 6.0 %fusion.78 = (bf16[32,256,256]{2,1,0:T(8,128)(2,1)}, bf16[32,256,256]{2,1,0:T(8,128)(2,1)}) fusion(bf16[32,256,512]{2,1,0:T(8,128)(2,1)} %param.41), kind=kLoop, calls=%fused_computation.203 | loop fusion | bytes 16777216 | tf_op jit(solution)/shard_map/slice | solution.py:164
  24.6 6.5 %copy.137 = bf16[32,256,256]{1,2,0:T(8,128)(2,1)} copy(bf16[32,256,256]{2,1,0:T(8,128)(2,1)} %get-tuple-element.233) | data formatting | bytes 8388608
  31.2 2.9 %fusion.79 = (f32[32,2,4]{2,1,0:T(2,128)S(1)}, f32[32,2,4,256]{3,2,1,0:T(4,128)S(1)}) fusion(bf16[32,2,4,128]{3,2,1,0:T(4,128)(2,1)S(1)} %reshape.219, bf16[32,256,2,128]{1,3,2,0:T(8,128)(2,1)} %bitcast.234, pred[32,256]{1,0:T(8,128)(4,1)S(1)} %fusion.51), kind=kOutput, calls=%fused_computation.204 | convolution fusion | flops 16973568 | bytes 4531200 | tf_op jit(solution)/shard_map/rkgd,rskd->rkgs/dot_general | solution.py:59
  35.8 1.4 copy.96
  37.2 1.7 fusion.37
  38.9 1.0 copy.84
  39.9 1.3 reshape.256
  41.3 1.6 fusion.80
  44.3 1.3 max.53
  45.6 1.3 add_convert_fusion
  51.2 1.4 copy.105
  52.6 6.5 %copy.138 = bf16[32,256,256]{1,2,0:T(8,128)(2,1)} copy(bf16[32,256,256]{2,1,0:T(8,128)(2,1)} %get-tuple-element.232) | data formatting | bytes 8388608
  59.1 1.4 fusion.14
  61.4 2.2 fusion.15
  63.6 6.4 %all-gather.2 = bf16[128,2,4,128]{3,2,1,0:T(4,128)(2,1)S(1)} all-gather(bf16[32,2,4,128]{3,2,1,0:T(4,128)(2,1)S(1)} %fusion.15), channel_id=4, replica_groups=mesh['req'=8,'tp'=4] {'tp'}, dimensions={0}, use_global_device_ids=true | all-gather | bytes 327680 | tf_op jit(solution)/shard_map/all_gather | solution.py:20
  71.4 5.4 %all-gather.1 = bf16[128,2,4]{2,1,0:T(2,128)(2,1)S(1)} all-gather(bf16[32,2,4]{2,1,0:T(2,128)(2,1)} %copy.97), channel_id=3, replica_groups=mesh['req'=8,'tp'=4] {'tp'}, dimensions={0}, use_global_device_ids=true | all-gather | bytes 2560 | tf_op jit(solution)/shard_map/all_gather | solution.py:20
  79.0 1.4 copy.90
  80.4 5.4 %all-gather = bf16[128,2,4]{2,1,0:T(2,128)(2,1)S(1)} all-gather(bf16[32,2,4]{2,1,0:T(2,128)(2,1)} %copy.90), channel_id=2, replica_groups=mesh['req'=8,'tp'=4] {'tp'}, dimensions={0}, use_global_device_ids=true | all-gather | bytes 2560 | tf_op jit(solution)/shard_map/all_gather | solution.py:20
  86.5 1.4 copy.108
  88.6 8.4 %while.19 = (s32[]{:T(128)}, f32[32,2,4]{0,2,1:T(4,128)}, f32[32,2,4]{0,2,1:T(4,128)S(1)}, f32[32,2,4,128]{3,2,1,0:T(4,128)S(1)}, bf16[4,32,2,4]{1,3,2,0:T(4,128...) while((s32[]{:T(128)}, f32[32,2,4]{0,2,1:T(4,128)}, ...), condition=%wide.region_8.9_spmd, body=%wide.region_7.8_spmd.sunk | while | flops 133125 | bytes 341143 | solution.py:28
  88.6 1.3 fusion.97
  90.1 1.3 fusion.98
  91.4 1.3 fusion.97
  92.9 1.3 fusion.98
  94.2 1.3 fusion.97
  95.7 1.3 fusion.98
  99.3 1.4 fusion.16
  103.0 1.0 convolution_convert_fusion.3
  106.1 1.3 fusion.19
  108.9 5.2 %all_gather.23 = bf16[32,512]{1,0:T(8,128)(2,1)S(1)} all-gather(bf16[32,128]{1,0:T(8,128)(2,1)S(1)} %fusion.60), channel_id=1, replica_groups=mesh['req'=8,'tp'=4] {'tp'}, dimensions={1}, use_global_device_ids=true | all-gather | bytes 40960 | tf_op jit(solution)/shard_map/all_gather | solution.py:126
  116.2 10.6 %fusion.4 = f32[32,1,6,64]{3,1,2,0:T(1,128)S(1)} fusion(bf16[32,6,64,256]{3,2,1,0:T(8,128)(2,1)} %param.37, f32[32,256]{1,0:T(8,128)} %get-tuple-element.239, f32[32,6,64]{2,1,0:T(8,128)S(1)} %broadcast_multiply_fusion, f32[32,6]{1,0:T(8,128)} %copy.81, bf16[32,256,1,1]{1,0,2,3:T(8,128)(2,1)} %get-tuple-element.238), kind=kOutput, calls=%fused_computation.10 | convolution fusion | flops 50331648 | bytes 6439680 | tf_op jit(solution)/shard_map/rhpn,rn->rhp/dot_general | solution.py:136
  127.5 1.0 reshape.218
  128.7 7.4 %psum.14 = f32[32]{0:T(128)S(1)} all-reduce(f32[32]{0:T(128)S(1)} %multiply_reduce_fusion.2), channel_id=1, replica_groups=mesh['req'=8,'tp'=4] {'tp'}, use_global_device_ids=true, to_apply=%region_2.3 | all-reduce | flops 32 | bytes 256 | tf_op jit(solution)/shard_map/psum | solution.py:143
  136.1 1.8 fusion.53
  137.9 2.2 fusion.10
  140.2 31.8 %all-reduce.2.cloned.1.call-done = bf16[32,2048]{1,0:T(8,128)(2,1)} async-done(((bf16[32,2048]{1,0:T(8,128)(2,1)}), bf16[32,2048]{1,0:T(8,128)(2,1)}) %all-reduce.2.cloned.1.call-update) | async-done | bytes 131088 | tf_op jit(solution)/shard_map/psum | solution.py:179
  172.0 1.1 fusion.20
  173.9 41.2 %all-gather.5.cloned.1.call-done = bf16[256,2048]{1,0:T(8,128)(2,1)} async-done(((bf16[32,2048]{1,0:T(8,128)(2,1)}), bf16[256,2048]{1,0:T(8,128)(2,1)}) %all-gather.5.cloned.1.call-update) | async-done | bytes 1048592 | tf_op jit(solution)/shard_map/all_gather | solution.py:184
  215.1 6.0 %convolution_convert_fusion = bf16[256,2048]{1,0:T(8,128)(2,1)S(1)} fusion(bf16[256,2048]{1,0:T(8,128)(2,1)} %all-gather.5.cloned.1.call-done, bf16[2048,2048]{1,0:T(8,128)(2,1)} %param.45), kind=kOutput, calls=%fused_computation.16 | convolution fusion | flops 2148007936 | bytes 10485760 | tf_op jit(solution)/shard_map/dot_general | solution.py:183
  240.9 3.5 %all-to-all-start = ((bf16[32,8,2048]{2,1,0:T(8,128)(2,1)}), bf16[32,8,2048]{2,1,0:T(8,128)(2,1)}, u32[]{:S(2)}, u32[]{:S(2)}) async-start(bf16[32,8,2048]{2,1,0:T(8,128)(2,1)} %constant_dynamic-update-slice_fusion), calls=%async_computation | async-start | bytes 2097152 | tf_op jit(solution)/shard_map/all_to_all | solution.py:189
  244.4 1.4 slice.85
  245.8 1.3 fusion.52
  247.8 8.1 %fusion.3 = bf16[32,6,64,256]{3,2,1,0:T(8,128)(2,1)} fusion(bf16[32,6,64,256]{3,2,1,0:T(8,128)(2,1)} %param.37, f32[32,256]{1,0:T(8,128)S(1)} %copy-done.11, f32[32,6,64]{2,1,0:T(8,128)S(1)} %copy-done.7, f32[32,6]{1,0:T(8,128)} %copy.81), kind=kLoop, calls=%fused_computation.9 | loop fusion | flops 15728640 | bytes 12665600 | tf_op jit(solution)/shard_map/convert_element_type | solution.py:139
  256.5 14.2 %all-to-all-done = bf16[32,8,2048]{2,1,0:T(8,128)(2,1)} async-done(((bf16[32,8,2048]{2,1,0:T(8,128)(2,1)}), bf16[32,8,2048]{2,1,0:T(8,128)(2,1)}, u32[]{:S(2)}, u32[]{:S(2)}) %all-to-all-start) | async-done | bytes 1048608 | tf_op jit(solution)/shard_map/all_to_all | solution.py:189
  270.6 2.8 convert_element_type.203
  (138 shorter events, 48.9 us)
Async XLA Ops:
  7.2 92.1 %copy-start = (bf16[2048,2,384]{2,1,0:T(2,128)(2,1)S(1)}, bf16[2048,2,384]{2,1,0:T(2,128)(2,1)}, u32[]{:S(2)}) copy-start(bf16[2048,2,384]{2,1,0:T(2,128)(2,1)} %param.27) | copy-start | bytes 9437188
  7.2 164.8 %all-reduce.2.cloned.1.call-start = ((), (), s32[]{:S(2)}) async-start(), calls=%async_computation.1 | async-start | bytes 262144 | tf_op jit(solution)/shard_map/psum | solution.py:179
  8.4 8.2 %copy-start.20 = (f32[32]{0:T(128)}, f32[32]{0:T(128)S(1)}, u32[]{:S(2)}) copy-start(f32[32]{0:T(128)S(1)} %add_rsqrt_fusion.2) | copy-start | bytes 388
  16.6 0.7 copy-start.5
  31.2 6.0 %copy-start.14 = (pred[32,256]{1,0:T(8,128)(4,1)}, pred[32,256]{1,0:T(8,128)(4,1)S(1)}, u32[]{:S(2)}) copy-start(pred[32,256]{1,0:T(8,128)(4,1)S(1)} %fusion.51) | copy-start | bytes 24580
  34.2 24.9 %copy-start.4 = (f32[32,2,4,256]{3,2,1,0:T(4,128)}, f32[32,2,4,256]{3,2,1,0:T(4,128)S(1)}, u32[]{:S(2)}) copy-start(f32[32,2,4,256]{3,2,1,0:T(4,128)S(1)} %get-tuple-element.246) | copy-start | bytes 786436
  51.2 7.9 %copy-start.16 = (f32[32,2,4]{2,1,0:T(2,128)S(1)}, f32[32,2,4]{2,1,0:T(2,128)}, u32[]{:S(2)}) copy-start(f32[32,2,4]{2,1,0:T(2,128)} %copy.100) | copy-start | bytes 3076
  52.6 7.9 %copy-start.15 = (pred[32,256]{1,0:T(8,128)(4,1)S(1)}, pred[32,256]{1,0:T(8,128)(4,1)}, u32[]{:S(2)}) copy-start(pred[32,256]{1,0:T(8,128)(4,1)} %copy-done.14) | copy-start | bytes 24580
  59.1 2.3 copy-start.1
  59.1 2.3 copy-start.17
  59.1 11.5 %copy-start.19 = (bf16[32,2,4]{0,2,1:T(4,128)(2,1)S(1)}, bf16[32,2,4]{0,2,1:T(4,128)(2,1)}, u32[]{:S(2)}) copy-start(bf16[32,2,4]{0,2,1:T(4,128)(2,1)} %get-tuple-element.228) | copy-start | bytes 1540
  60.5 38.8 %copy-start.2 = (bf16[32,2048]{1,0:T(8,128)(2,1)S(1)}, bf16[32,2048]{1,0:T(8,128)(2,1)}, u32[]{:S(2)}) copy-start(bf16[32,2048]{1,0:T(8,128)(2,1)} %param.24) | copy-start | bytes 393220
  63.6 37.8 %copy-start.8 = (bf16[32,3,384]{2,0,1:T(8,128)(2,1)S(1)}, bf16[32,3,384]{2,0,1:T(8,128)(2,1)}, u32[]{:S(2)}) copy-start(bf16[32,3,384]{2,0,1:T(8,128)(2,1)} %param.33) | copy-start | bytes 221188
  69.9 0.7 copy-start.3
  100.7 26.1 %copy-start.9 = (bf16[32,1,384]{2,0,1:T(8,128)(2,1)}, bf16[32,1,384]{2,0,1:T(8,128)(2,1)S(1)}, u32[]{:S(2)}) copy-start(bf16[32,1,384]{2,0,1:T(8,128)(2,1)S(1)} %get-tuple-element.237) | copy-start | bytes 73732
  107.4 19.4 %copy-start.12 = (bf16[32,1,128]{2,0,1:T(8,128)(2,1)}, bf16[32,1,128]{2,0,1:T(8,128)(2,1)S(1)}, u32[]{:S(2)}) copy-start(bf16[32,1,128]{2,0,1:T(8,128)(2,1)S(1)} %fusion.19) | copy-start | bytes 24580
  116.2 10.6 %copy-start.6 = (f32[32,6,64]{2,1,0:T(8,128)}, f32[32,6,64]{2,1,0:T(8,128)S(1)}, u32[]{:S(2)}) copy-start(f32[32,6,64]{2,1,0:T(8,128)S(1)} %broadcast_multiply_fusion) | copy-start | bytes 147460
  116.2 10.6 %copy-start.22 = (f32[6]{0:T(128)S(1)}, f32[6]{0:T(128)}, u32[]{:S(2)}) copy-start(f32[6]{0:T(128)} %param.31) | copy-start | bytes 76
  116.2 19.9 %copy-start.21 = (f32[384]{0:T(512)S(1)}, f32[384]{0:T(512)}, u32[]{:S(2)}) copy-start(f32[384]{0:T(512)} %param.38) | copy-start | bytes 4612
  116.2 56.9 %copy-start.18 = (f32[2048]{0:T(1024)S(1)}, f32[2048]{0:T(1024)}, u32[]{:S(2)}) copy-start(f32[2048]{0:T(1024)} %param.44) | copy-start | bytes 24580
  140.1 75.0 %all-gather.5.cloned.1.call-start = ((), (), s32[]{:S(2)}) async-start(), calls=%async_computation.2 | async-start | bytes 1179648 | tf_op jit(solution)/shard_map/all_gather | solution.py:184
  173.9 71.9 %copy-start.13 = (bf16[32,1,128]{2,0,1:T(8,128)(2,1)S(1)}, bf16[32,1,128]{2,0,1:T(8,128)(2,1)}, u32[]{:S(2)}) copy-start(bf16[32,1,128]{2,0,1:T(8,128)(2,1)} %copy-done.12) | copy-start | bytes 24580
  173.9 73.2 %copy-start.10 = (bf16[32,1,384]{2,0,1:T(8,128)(2,1)S(1)}, bf16[32,1,384]{2,0,1:T(8,128)(2,1)}, u32[]{:S(2)}) copy-start(bf16[32,1,384]{2,0,1:T(8,128)(2,1)} %copy-done.9) | copy-start | bytes 73732
  173.9 73.9 %copy-start.7 = (f32[32,6,64]{2,1,0:T(8,128)S(1)}, f32[32,6,64]{2,1,0:T(8,128)}, u32[]{:S(2)}) copy-start(f32[32,6,64]{2,1,0:T(8,128)} %copy-done.6) | copy-start | bytes 147460
  173.9 73.9 %copy-start.11 = (f32[32,256]{1,0:T(8,128)S(1)}, f32[32,256]{1,0:T(8,128)}, u32[]{:S(2)}) copy-start(f32[32,256]{1,0:T(8,128)} %get-tuple-element.239) | copy-start | bytes 98308
  240.9 29.7 %all-to-all-start = ((bf16[32,8,2048]{2,1,0:T(8,128)(2,1)}), bf16[32,8,2048]{2,1,0:T(8,128)(2,1)}, u32[]{:S(2)}, u32[]{:S(2)}) async-start(bf16[32,8,2048]{2,1,0:T(8,128)(2,1)} %constant_dynamic-update-slice_fusion), calls=%async_computation | async-start | bytes 2097152 | tf_op jit(solution)/shard_map/all_to_all | solution.py:189
Sparse Core Ops, SparseCore 0:
  140.2 31.7 all-reduce.1
  174.9 40.1 all-gather.4
